TPU v7x, 32 devices: a whole 2x2x4 slice. The times are simulated.
32 devices in a mesh: groups: 2 (over y), prow: 4 (over x, core), pcol: 4 (over z).
Axes of the slice: x: 2, y: 2, z: 4, core: 2. Of those that a mesh axis runs over, the one named last changes fastest.
Arguments:
- anc_inverse: float32 [4096, 2048], P(('groups', 'prow'), 'pcol'), parts along dimension 0
- anc_factor: float32 [8, 2048, 256], P('groups', ('prow', 'pcol')), parts along dimension 0, may hold values from -0.0625 to 0.0625
- win_factor: float32 [12, 256, 256], P('groups'), parts along dimension 0, may hold values from -0.1875 to 0.1875
- diag_inverse: float32 [8, 256, 256], P('groups'), parts along dimension 0
- first_reader: int32 [32], P('groups'), parts along dimension 0, may hold values from 0 to 4
Outputs:
- anc_panels: float32 [8, 2048, 256], P('groups', ('prow', 'pcol')), parts along dimension 0
- window_inverse: float32 [8, 4, 256, 256], P('groups'), parts along dimension 0
There are 2 independent parts, one for each index of `groups`. A program takes and returns all parts, laid end to end along the dimension named above; each array names one. Nothing has to cross between parts.
Inputs may be any that keep to these rules, and one draw needn't show every extreme that they name: Ancestor block b belongs to the pattern of supernode k exactly when first_reader[b] <= k; the value 4 puts it in no pattern, so patterns grow with k. Within each part, anc_inverse is symmetric: anc_inverse[r, s] = anc_inverse[s, r].
All inputs are finite; a program needn't handle non-finite values.
Results may differ from a plain program's by a relative error of at most 0.0003.
Values sent between devices are 32-bit elements; how exact they have to be, the bound alone decides.
A program may use at most 64 MiB of HBM per device.

v0:
```python
import jax
import jax.numpy as jnp
from jax import lax
from jax.sharding import PartitionSpec as P

BLK = 128


def broadcast(array, axis, root):
    mine = lax.axis_index(axis) == root
    return lax.psum(jnp.where(mine, array, jnp.zeros_like(array)), axis)


def to_columns(stacked, per_column, pcol_at):
    gathered = lax.all_gather(stacked, "pcol", axis=1, tiled=True)
    pieces = [
        broadcast(gathered, "prow", pcol_at * per_column + offset) for offset in range(per_column)
    ]
    return jnp.concatenate(pieces, axis=1)


def window_algebra(summed, upper_all, diag_inverse, window_count):
    highest = lax.Precision.HIGHEST
    blocks = [[None] * window_count for column in range(window_count)]
    for node in reversed(range(window_count)):
        linv = diag_inverse[node]
        later = list(range(node + 1, window_count))
        upper_u = upper_all[node]
        cross = {}
        for position, other in enumerate(later):
            term = summed[node][position]
            for second in later:
                term = term + jnp.dot(blocks[other][second], upper_u[second], precision=highest)
            cross[other] = term
        own = jnp.dot(linv.T, linv, precision=highest) + summed[node][len(later)]
        for other in later:
            own = own + jnp.dot(upper_u[other].T, cross[other], precision=highest)
        blocks[node][node] = own
        for other in later:
            blocks[other][node] = -cross[other]
            blocks[node][other] = -cross[other].T
    return jnp.stack([jnp.stack(blocks[row_at]) for row_at in range(window_count)])


def per_device(anc_inverse, anc_factor, win_factor, diag_inverse, first_reader):
    highest = lax.Precision.HIGHEST
    n_prow = lax.axis_size("prow")
    n_pcol = lax.axis_size("pcol")
    per_column = n_prow // n_pcol
    prow_at = lax.axis_index("prow")
    pcol_at = lax.axis_index("pcol")
    window_count = diag_inverse.shape[0]
    fine_rows = anc_factor.shape[1]
    start_row = (prow_at * n_pcol + pcol_at) * fine_rows
    block_of = (start_row + jnp.arange(fine_rows, dtype=jnp.int32)) // BLK
    block_ids = jnp.arange(first_reader.shape[0], dtype=jnp.int32)
    readers = jnp.sum(
        jnp.where(block_of[:, None] == block_ids[None, :], first_reader[None, :], 0), axis=1
    )
    row_masks = [(readers <= node).astype(jnp.float32)[:, None] for node in range(window_count)]
    lower_all = [
        jnp.dot(anc_factor[node], diag_inverse[node], precision=highest) * row_masks[node]
        for node in range(window_count)
    ]
    whole = to_columns(jnp.stack(lower_all), per_column, pcol_at)
    column_panels = [whole[node] for node in range(window_count)]
    panels = [None] * window_count
    upper_all = [None] * window_count
    summed = [None] * window_count
    for node in reversed(range(window_count)):
        linv = diag_inverse[node]
        later = list(range(node + 1, window_count))
        upper_u = {}
        for other in later:
            upper_u[other] = jnp.dot(
                win_factor[other * (other - 1) // 2 + node], linv, precision=highest
            )
        upper_all[node] = upper_u
        columns = column_panels[node]
        full_x = lax.psum_scatter(
            jnp.dot(anc_inverse, columns, precision=highest),
            "pcol",
            scatter_dimension=0,
            tiled=True,
        )
        for other in later:
            full_x = full_x + jnp.dot(panels[other], upper_u[other], precision=highest)
        partials = [jnp.dot(panels[other].T, lower_all[node], precision=highest) for other in later]
        partials.append(jnp.dot(lower_all[node].T, full_x, precision=highest))
        panels[node] = -full_x * row_masks[node]
        summed[node] = list(lax.psum(tuple(partials), ("prow", "pcol")))
    window_inverse = window_algebra(summed, upper_all, diag_inverse, window_count)
    return (jnp.stack(panels), window_inverse)


def solution(mesh):
    return jax.shard_map(
        per_device,
        mesh=mesh,
        in_specs=(
            P(("groups", "prow"), "pcol"),
            P("groups", ("prow", "pcol"), None),
            P("groups", None, None),
            P("groups", None, None),
            P("groups"),
        ),
        out_specs=(P("groups", ("prow", "pcol"), None), P("groups", None, None, None)),
        check_vma=False,
    )
```

profile of v0, /device:TPU:0, one launch (start us, length us, event | category | flops | bytes accessed | tf_op | source)
XLA Modules:
  0.0 358.3 jit_solution(12927005311065160913)
XLA Ops:
  12.1 1.3 convolution_multiply_fusion
  14.4 48.7 %all-gather.2.cloned.1.call-done = f32[4,512,256]{2,1,0:T(8,128)} async-done(((f32[4,128,256]{2,1,0:T(8,128)}), f32[4,512,256]{2,1,0:T(8,128)}) %all-gather.2.cloned.1.call-update) | async-done | bytes 2097168 | tf_op jit(solution)/shard_map/all_gather | solution.py:15
  63.2 3.1 broadcast_select_fusion
  66.3 50.1 %all-reduce.4.cloned.1.call-done = f32[4,512,256]{2,1,0:T(8,128)} async-done(((f32[4,512,256]{2,1,0:T(8,128)}), f32[4,512,256]{2,1,0:T(8,128)}) %all-reduce.4.cloned.1.call-update) | async-done | bytes 2097168 | tf_op jit(solution)/shard_map/psum | solution.py:11
  116.4 2.8 convolution_bitcast_fusion
  119.4 2.9 convolution_bitcast_fusion.1
  125.0 2.9 convolution_bitcast_fusion.2
  132.0 2.1 fusion.11
  134.1 2.9 convolution_bitcast_fusion.3
  137.2 4.0 %reduce-scatter.11.cloned.1.call-done = f32[128,256]{1,0:T(8,128)} async-done(((f32[512,256]{1,0:T(8,128)}), f32[128,256]{1,0:T(8,128)}) %reduce-scatter.11.cloned.1.call-update) | async-done | bytes 131088 | tf_op jit(solution)/shard_map/reduce_scatter | solution.py:80
  141.2 22.7 %reduce-scatter.9.cloned.1.call-done = f32[128,256]{1,0:T(8,128)} async-done(((f32[512,256]{1,0:T(8,128)}), f32[128,256]{1,0:T(8,128)}) %reduce-scatter.9.cloned.1.call-update) | async-done | bytes 131088 | tf_op jit(solution)/shard_map/reduce_scatter | solution.py:80
  163.9 1.4 convolution_add_fusion.29
  165.3 20.7 %reduce-scatter.7.cloned.1.call-done = f32[128,256]{1,0:T(8,128)} async-done(((f32[512,256]{1,0:T(8,128)}), f32[128,256]{1,0:T(8,128)}) %reduce-scatter.7.cloned.1.call-update) | async-done | bytes 131088 | tf_op jit(solution)/shard_map/reduce_scatter | solution.py:80
  188.5 2.2 fusion.80
  190.7 2.0 fusion.79
  192.7 2.1 fusion.66
  194.8 2.1 fusion.65
  198.0 10.0 %reduce-scatter.5.cloned.1.call-done = f32[128,256]{1,0:T(8,128)} async-done(((f32[512,256]{1,0:T(8,128)}), f32[128,256]{1,0:T(8,128)}) %reduce-scatter.5.cloned.1.call-update) | async-done | bytes 131088 | tf_op jit(solution)/shard_map/reduce_scatter | solution.py:80
  211.0 2.1 fusion.78
  220.8 99.6 %all-reduce.6.cloned.1.call-done = (f32[256,256]{1,0:T(8,128)}, f32[256,256]{1,0:T(8,128)}, f32[256,256]{0,1:T(8,128)}, f32[256,256]{1,0:T(8,128)}, f32[256,256]...) async-done(((f32[256,256]{1,0:T(8,128)}, f32[256,256]{1,0:T(8,128)}, ...) | async-done | bytes 2621456 | tf_op jit(solution)/shard_map/psum | solution.py:91
  320.3 1.5 convolution_add_fusion.20
  321.9 1.5 convolution_add_fusion.19
  323.4 1.5 convolution_add_fusion.14
  349.0 2.4 pad_maximum_fusion
  (147 shorter events, 50.8 us)
Async XLA Ops:
  7.2 109.3 %copy-start = (f32[512,512]{1,0:T(8,128)S(1)}, f32[512,512]{1,0:T(8,128)}, u32[]{:S(2)}) copy-start(f32[512,512]{1,0:T(8,128)} %param.5) | copy-start | bytes 3145732
  7.2 56.0 %all-gather.2.cloned.1.call-start = ((), (), s32[]{:S(2)}) async-start(), calls=%async_computation.4 | async-start | bytes 2621440 | tf_op jit(solution)/shard_map/all_gather | solution.py:15
  9.4 56.9 %copy-start.6 = (f32[128,256]{1,0:T(8,128)}, f32[128,256]{1,0:T(8,128)S(1)}, u32[]{:S(2)}) copy-start(f32[128,256]{1,0:T(8,128)S(1)} %convolution_multiply_fusion.3) | copy-start | bytes 393220
  10.7 55.5 %copy-start.13 = (f32[128,256]{1,0:T(8,128)}, f32[128,256]{1,0:T(8,128)S(1)}, u32[]{:S(2)}) copy-start(f32[128,256]{1,0:T(8,128)S(1)} %convolution_multiply_fusion.2) | copy-start | bytes 393220
  12.1 54.1 %copy-start.17 = (f32[128,256]{1,0:T(8,128)}, f32[128,256]{1,0:T(8,128)S(1)}, u32[]{:S(2)}) copy-start(f32[128,256]{1,0:T(8,128)S(1)} %convolution_multiply_fusion.1) | copy-start | bytes 393220
  13.5 52.8 %copy-start.19 = (f32[128,256]{1,0:T(8,128)}, f32[128,256]{1,0:T(8,128)S(1)}, u32[]{:S(2)}) copy-start(f32[128,256]{1,0:T(8,128)S(1)} %convolution_multiply_fusion) | copy-start | bytes 393220
  14.4 102.1 %all-reduce.4.cloned.1.call-start = ((), (), s32[]{:S(2)}) async-start(), calls=%async_computation.5 | async-start | bytes 4194304 | tf_op jit(solution)/shard_map/psum | solution.py:11
  66.3 74.9 %reduce-scatter.11.cloned.1.call-start = ((), (), s32[]{:S(2)}) async-start(), calls=%async_computation.9 | async-start | bytes 655360 | tf_op jit(solution)/shard_map/reduce_scatter | solution.py:80
  119.3 44.6 %reduce-scatter.9.cloned.1.call-start = ((), (), s32[]{:S(2)}) async-start(), calls=%async_computation.8 | async-start | bytes 655360 | tf_op jit(solution)/shard_map/reduce_scatter | solution.py:80
  122.3 63.7 %reduce-scatter.7.cloned.1.call-start = ((), (), s32[]{:S(2)}) async-start(), calls=%async_computation.7 | async-start | bytes 655360 | tf_op jit(solution)/shard_map/reduce_scatter | solution.py:80
  127.9 80.1 %reduce-scatter.5.cloned.1.call-start = ((), (), s32[]{:S(2)}) async-start(), calls=%async_computation.6 | async-start | bytes 655360 | tf_op jit(solution)/shard_map/reduce_scatter | solution.py:80
  137.0 183.4 %all-reduce.6.cloned.1.call-start = ((), (), s32[]{:S(2)}) async-start(), calls=%async_computation.10 | async-start | bytes 5242880 | tf_op jit(solution)/shard_map/psum | solution.py:91
  165.2 22.0 %copy-start.5 = (f32[128,256]{1,0:T(8,128)}, f32[128,256]{1,0:T(8,128)S(1)}, u32[]{:S(2)}) copy-start(f32[128,256]{1,0:T(8,128)S(1)} %convolution_add_fusion.29) | copy-start | bytes 393220
  186.0 6.7 %copy-start.14 = (f32[128,256]{1,0:T(8,128)S(1)}, f32[128,256]{1,0:T(8,128)}, u32[]{:S(2)}) copy-start(f32[128,256]{1,0:T(8,128)} %copy-done.13) | copy-start | bytes 393220
  186.0 8.8 %copy-start.7 = (f32[128,256]{1,0:T(8,128)S(1)}, f32[128,256]{1,0:T(8,128)}, u32[]{:S(2)}) copy-start(f32[128,256]{1,0:T(8,128)} %copy-done.6) | copy-start | bytes 393220
  188.5 8.4 %copy-start.16 = (f32[128,256]{1,0:T(8,128)}, f32[128,256]{1,0:T(8,128)S(1)}, u32[]{:S(2)}) copy-start(f32[128,256]{1,0:T(8,128)S(1)} %convolution_add_fusion.27) | copy-start | bytes 393220
  188.5 22.2 %copy-start.2 = (f32[128,256]{1,0:T(8,128)S(1)}, f32[128,256]{1,0:T(8,128)}, u32[]{:S(2)}) copy-start(f32[128,256]{1,0:T(8,128)} %reduce-scatter.11.cloned.1.call-done) | copy-start | bytes 393220
  208.1 5.0 %copy-start.20 = (f32[128,256]{1,0:T(8,128)S(1)}, f32[128,256]{1,0:T(8,128)}, u32[]{:S(2)}) copy-start(f32[128,256]{1,0:T(8,128)} %copy-done.19) | copy-start | bytes 393220
  208.1 6.1 %copy-start.18 = (f32[128,256]{1,0:T(8,128)S(1)}, f32[128,256]{1,0:T(8,128)}, u32[]{:S(2)}) copy-start(f32[128,256]{1,0:T(8,128)} %copy-done.17) | copy-start | bytes 393220
  208.1 7.3 %copy-start.15 = (f32[128,256]{1,0:T(8,128)S(1)}, f32[128,256]{1,0:T(8,128)}, u32[]{:S(2)}) copy-start(f32[128,256]{1,0:T(8,128)} %copy-done.13) | copy-start | bytes 393220
  208.1 8.5 %copy-start.8 = (f32[128,256]{1,0:T(8,128)S(1)}, f32[128,256]{1,0:T(8,128)}, u32[]{:S(2)}) copy-start(f32[128,256]{1,0:T(8,128)} %copy-done.6) | copy-start | bytes 393220
  211.0 5.6 %copy-start.21 = (f32[128,256]{1,0:T(8,128)}, f32[128,256]{1,0:T(8,128)S(1)}, u32[]{:S(2)}) copy-start(f32[128,256]{1,0:T(8,128)S(1)} %convolution_add_fusion.24) | copy-start | bytes 393220
  321.9 5.6 %copy-start.3 = (f32[256,256]{1,0:T(8,128)}, f32[256,256]{1,0:T(8,128)S(1)}, u32[]{:S(2)}) copy-start(f32[256,256]{1,0:T(8,128)S(1)} %convolution_add_fusion.20) | copy-start | bytes 786436
  339.0 4.8 %copy-start.12 = (f32[256,256]{0,1:T(8,128)S(1)}, f32[256,256]{0,1:T(8,128)}, u32[]{:S(2)}) copy-start(f32[256,256]{0,1:T(8,128)} %copy-done.11) | copy-start | bytes 786436
  (20 other events, 45.0 us)
Sparse Core Ops, SparseCore 0:
  14.5 48.6 all-gather.1
  66.4 49.9 all-reduce.3
  119.4 21.7 reduce-scatter.10
  144.0 19.8 reduce-scatter.8
  166.1 19.8 reduce-scatter.6
  188.2 19.8 reduce-scatter.4
  217.9 102.3 all-reduce.5
where the time goes:
time: 359 us; the launch traced here: 358 us
  waiting for transfers between devices  256 us (71%)
  matrix products  65.6 us (18%)
  other arithmetic  16.4 us (5%)
  between operations  14.9 us (4%)
  local copies, waits for them, and re-layouts  5.02 us (1%)
    psum x1, waiting for transfers between devices, per_device(): summed[node] = list(lax.psum(tuple(partials), ('prow', 'pcol')))  99.6 us
    reduce_scatter x4, waiting for transfers between devices, per_device(): lax.psum_scatter(jnp.dot(anc_inverse, columns, precision=highest), 'pcol'...  57.4 us
    psum x1, waiting for transfers between devices, broadcast(): return lax.psum(jnp.where(mine, array, jnp.zeros_like(array)), axis)  50.1 us
    all_gather x1, waiting for transfers between devices, to_columns(): gathered = lax.all_gather(stacked, 'pcol', axis=1, tiled=True)  48.7 us
    dot_general x4, matrix products, per_device(): jnp.dot(anc_inverse, columns, precision=highest)  11.5 us
    dot_general x14, matrix products, window_algebra(): jnp.dot(blocks[other][second], upper_u[second], precision=highest)  9.39 us
    dot_general x6, matrix products, per_device(): jnp.dot(panels[other].T, lower_all[node], precision=highest)  8.88 us
    dot_general x6, matrix products, per_device(): jnp.dot(win_factor[other * (other - 1) // 2 + node], linv, precision=high...  8.71 us
  transfers between devices with their start and end apart: 7, of which 7 were waited for; matrix products, arithmetic and copies ran while one was open for 9% of the time, Pallas kernels for 0%

commit v1 on v0

--- a/solution.py
+++ b/solution.py
@@ -88,7 +88,7 @@
         partials = [jnp.dot(panels[other].T, lower_all[node], precision=highest) for other in later]
         partials.append(jnp.dot(lower_all[node].T, full_x, precision=highest))
         panels[node] = -full_x * row_masks[node]
-        summed[node] = list(lax.psum(tuple(partials), ("prow", "pcol")))
+        summed[node] = list(lax.psum(lax.psum(tuple(partials), "pcol"), "prow"))
     window_inverse = window_algebra(summed, upper_all, diag_inverse, window_count)
     return (jnp.stack(panels), window_inverse)
 

time: 359 us -> 425 us (1.18)
  waiting for transfers between devices: 256 us -> 323 us
    psum x1 -> x2, waiting for transfers between devices: 99.6 us -> 166 us  [per_device(): summed[node] = list(lax.psum(lax.psum(tuple(partials), 'pcol'), 'prow'))]
  transfers between devices with their start and end apart: 7 -> 8, of which waited for: 7 -> 8; matrix products, arithmetic and copies ran while one was open for 9% -> 8% of each run, Pallas kernels for 0% -> 0%
where the time goes in v1:
time: 425 us; the launch traced here: 424 us
  waiting for transfers between devices  323 us (76%)
  matrix products  65.6 us (15%)
  other arithmetic  16.4 us (4%)
  between operations  14.9 us (4%)
    psum x2, waiting for transfers between devices, per_device(): summed[node] = list(lax.psum(lax.psum(tuple(partials), 'pcol'), 'prow'))  166 us
    reduce_scatter x4, waiting for transfers between devices, per_device(): lax.psum_scatter(jnp.dot(anc_inverse, columns, precision=highest), 'pcol'...  57.6 us
    psum x1, waiting for transfers between devices, broadcast(): return lax.psum(jnp.where(mine, array, jnp.zeros_like(array)), axis)  50.1 us
    all_gather x1, waiting for transfers between devices, to_columns(): gathered = lax.all_gather(stacked, 'pcol', axis=1, tiled=True)  48.7 us
    dot_general x4, matrix products, per_device(): jnp.dot(anc_inverse, columns, precision=highest)  11.5 us
    dot_general x14, matrix products, window_algebra(): jnp.dot(blocks[other][second], upper_u[second], precision=highest)  9.18 us
    dot_general x6, matrix products, per_device(): jnp.dot(panels[other].T, lower_all[node], precision=highest)  8.88 us
    dot_general x6, matrix products, per_device(): jnp.dot(win_factor[other * (other - 1) // 2 + node], linv, precision=high...  8.7 us
  transfers between devices with their start and end apart: 8, of which 8 were waited for; matrix products, arithmetic and copies ran while one was open for 8% of the time, Pallas kernels for 0%

profile of v1, /device:TPU:0, one launch (start us, length us, event | category | flops | bytes accessed | tf_op | source)
XLA Modules:
  0.0 423.6 jit_solution(3699055105803748396)
XLA Ops:
  14.4 48.7 %all-gather.2.cloned.1.call-done = f32[4,512,256]{2,1,0:T(8,128)} async-done(((f32[4,128,256]{2,1,0:T(8,128)}), f32[4,512,256]{2,1,0:T(8,128)}) %all-gather.2.cloned.1.call-update) | async-done | bytes 2097168 | tf_op jit(solution)/shard_map/all_gather | solution.py:15
  63.1 3.1 broadcast_select_fusion
  66.3 50.1 %all-reduce.6.cloned.1.call-done = f32[4,512,256]{2,1,0:T(8,128)} async-done(((f32[4,512,256]{2,1,0:T(8,128)}), f32[4,512,256]{2,1,0:T(8,128)}) %all-reduce.6.cloned.1.call-update) | async-done | bytes 2097168 | tf_op jit(solution)/shard_map/psum | solution.py:11
  116.4 2.8 convolution_bitcast_fusion
  119.3 2.9 convolution_bitcast_fusion.1
  125.0 2.9 convolution_bitcast_fusion.2
  132.0 2.0 fusion.11
  134.0 2.9 convolution_bitcast_fusion.3
  137.1 4.0 reduce-scatter.11.cloned.1.call-done
  141.2 22.8 %reduce-scatter.9.cloned.1.call-done = f32[128,256]{1,0:T(8,128)} async-done(((f32[512,256]{1,0:T(8,128)}), f32[128,256]{1,0:T(8,128)}) %reduce-scatter.9.cloned.1.call-update) | async-done | bytes 131088 | tf_op jit(solution)/shard_map/reduce_scatter | solution.py:80
  163.9 1.4 convolution_add_fusion.29
  165.3 20.7 %reduce-scatter.7.cloned.1.call-done = f32[128,256]{1,0:T(8,128)} async-done(((f32[512,256]{1,0:T(8,128)}), f32[128,256]{1,0:T(8,128)}) %reduce-scatter.7.cloned.1.call-update) | async-done | bytes 131088 | tf_op jit(solution)/shard_map/reduce_scatter | solution.py:80
  188.6 2.2 fusion.80
  190.7 2.0 fusion.79
  192.7 2.1 fusion.66
  194.8 2.1 fusion.65
  198.1 10.1 %reduce-scatter.5.cloned.1.call-done = f32[128,256]{1,0:T(8,128)} async-done(((f32[512,256]{1,0:T(8,128)}), f32[128,256]{1,0:T(8,128)}) %reduce-scatter.5.cloned.1.call-update) | async-done | bytes 131088 | tf_op jit(solution)/shard_map/reduce_scatter | solution.py:80
  211.1 2.1 fusion.78
  218.2 105.6 %all-reduce.8.cloned.1.call-done = (f32[256,256]{1,0:T(8,128)}, f32[256,256]{1,0:T(8,128)}, f32[256,256]{0,1:T(8,128)}, f32[256,256]{1,0:T(8,128)}, f32[256,256]...) async-done(((f32[256,256]{1,0:T(8,128)}, f32[256,256]{1,0:T(8,128)}, ...) | async-done | bytes 2621456 | tf_op jit(solution)/shard_map/psum | solution.py:91
  326.7 60.7 %all-reduce.10.cloned.1.call-done = (f32[256,256]{1,0:T(8,128)}, f32[256,256]{1,0:T(8,128)}, f32[256,256]{0,1:T(8,128)}, f32[256,256]{1,0:T(8,128)}, f32[256,256...) async-done(((f32[256,256]{1,0:T(8,128)}, f32[256,256]{1,0:T(8,128)}, ...) | async-done | bytes 2621456 | tf_op jit(solution)/shard_map/psum | solution.py:91
  387.4 1.5 convolution_add_fusion.20
  389.0 1.5 convolution_add_fusion.19
  390.5 1.5 convolution_add_fusion.14
  414.4 2.4 pad_maximum_fusion
  (152 shorter events, 50.7 us)
Async XLA Ops:
  7.2 109.3 %copy-start = (f32[512,512]{1,0:T(8,128)S(1)}, f32[512,512]{1,0:T(8,128)}, u32[]{:S(2)}) copy-start(f32[512,512]{1,0:T(8,128)} %param.5) | copy-start | bytes 3145732
  7.2 56.0 %all-gather.2.cloned.1.call-start = ((), (), s32[]{:S(2)}) async-start(), calls=%async_computation.4 | async-start | bytes 2621440 | tf_op jit(solution)/shard_map/all_gather | solution.py:15
  9.4 56.8 %copy-start.6 = (f32[128,256]{1,0:T(8,128)}, f32[128,256]{1,0:T(8,128)S(1)}, u32[]{:S(2)}) copy-start(f32[128,256]{1,0:T(8,128)S(1)} %convolution_multiply_fusion.3) | copy-start | bytes 393220
  10.7 55.5 %copy-start.12 = (f32[128,256]{1,0:T(8,128)}, f32[128,256]{1,0:T(8,128)S(1)}, u32[]{:S(2)}) copy-start(f32[128,256]{1,0:T(8,128)S(1)} %convolution_multiply_fusion.2) | copy-start | bytes 393220
  12.1 54.1 %copy-start.18 = (f32[128,256]{1,0:T(8,128)}, f32[128,256]{1,0:T(8,128)S(1)}, u32[]{:S(2)}) copy-start(f32[128,256]{1,0:T(8,128)S(1)} %convolution_multiply_fusion.1) | copy-start | bytes 393220
  13.5 52.8 %copy-start.20 = (f32[128,256]{1,0:T(8,128)}, f32[128,256]{1,0:T(8,128)S(1)}, u32[]{:S(2)}) copy-start(f32[128,256]{1,0:T(8,128)S(1)} %convolution_multiply_fusion) | copy-start | bytes 393220
  14.3 102.1 %all-reduce.6.cloned.1.call-start = ((), (), s32[]{:S(2)}) async-start(), calls=%async_computation.5 | async-start | bytes 4194304 | tf_op jit(solution)/shard_map/psum | solution.py:11
  66.3 74.9 %reduce-scatter.11.cloned.1.call-start = ((), (), s32[]{:S(2)}) async-start(), calls=%async_computation.9 | async-start | bytes 655360 | tf_op jit(solution)/shard_map/reduce_scatter | solution.py:80
  119.3 44.6 %reduce-scatter.9.cloned.1.call-start = ((), (), s32[]{:S(2)}) async-start(), calls=%async_computation.8 | async-start | bytes 655360 | tf_op jit(solution)/shard_map/reduce_scatter | solution.py:80
  122.3 63.8 %reduce-scatter.7.cloned.1.call-start = ((), (), s32[]{:S(2)}) async-start(), calls=%async_computation.7 | async-start | bytes 655360 | tf_op jit(solution)/shard_map/reduce_scatter | solution.py:80
  127.9 80.2 %reduce-scatter.5.cloned.1.call-start = ((), (), s32[]{:S(2)}) async-start(), calls=%async_computation.6 | async-start | bytes 655360 | tf_op jit(solution)/shard_map/reduce_scatter | solution.py:80
  136.9 186.8 %all-reduce.8.cloned.1.call-start = ((), (), s32[]{:S(2)}) async-start(), calls=%async_computation.10 | async-start | bytes 5242880 | tf_op jit(solution)/shard_map/psum | solution.py:91
  165.3 22.0 %copy-start.5 = (f32[128,256]{1,0:T(8,128)}, f32[128,256]{1,0:T(8,128)S(1)}, u32[]{:S(2)}) copy-start(f32[128,256]{1,0:T(8,128)S(1)} %convolution_add_fusion.29) | copy-start | bytes 393220
  186.0 6.7 %copy-start.13 = (f32[128,256]{1,0:T(8,128)S(1)}, f32[128,256]{1,0:T(8,128)}, u32[]{:S(2)}) copy-start(f32[128,256]{1,0:T(8,128)} %copy-done.12) | copy-start | bytes 393220
  186.0 8.8 %copy-start.7 = (f32[128,256]{1,0:T(8,128)S(1)}, f32[128,256]{1,0:T(8,128)}, u32[]{:S(2)}) copy-start(f32[128,256]{1,0:T(8,128)} %copy-done.6) | copy-start | bytes 393220
  188.5 8.3 %copy-start.15 = (f32[128,256]{1,0:T(8,128)}, f32[128,256]{1,0:T(8,128)S(1)}, u32[]{:S(2)}) copy-start(f32[128,256]{1,0:T(8,128)S(1)} %convolution_add_fusion.27) | copy-start | bytes 393220
  188.6 22.2 %copy-start.2 = (f32[128,256]{1,0:T(8,128)S(1)}, f32[128,256]{1,0:T(8,128)}, u32[]{:S(2)}) copy-start(f32[128,256]{1,0:T(8,128)} %reduce-scatter.11.cloned.1.call-done) | copy-start | bytes 393220
  208.1 5.0 %copy-start.21 = (f32[128,256]{1,0:T(8,128)S(1)}, f32[128,256]{1,0:T(8,128)}, u32[]{:S(2)}) copy-start(f32[128,256]{1,0:T(8,128)} %copy-done.20) | copy-start | bytes 393220
  208.2 6.1 %copy-start.19 = (f32[128,256]{1,0:T(8,128)S(1)}, f32[128,256]{1,0:T(8,128)}, u32[]{:S(2)}) copy-start(f32[128,256]{1,0:T(8,128)} %copy-done.18) | copy-start | bytes 393220
  208.2 7.3 %copy-start.14 = (f32[128,256]{1,0:T(8,128)S(1)}, f32[128,256]{1,0:T(8,128)}, u32[]{:S(2)}) copy-start(f32[128,256]{1,0:T(8,128)} %copy-done.12) | copy-start | bytes 393220
  208.2 8.5 %copy-start.8 = (f32[128,256]{1,0:T(8,128)S(1)}, f32[128,256]{1,0:T(8,128)}, u32[]{:S(2)}) copy-start(f32[128,256]{1,0:T(8,128)} %copy-done.6) | copy-start | bytes 393220
  211.1 5.6 %copy-start.22 = (f32[128,256]{1,0:T(8,128)}, f32[128,256]{1,0:T(8,128)S(1)}, u32[]{:S(2)}) copy-start(f32[128,256]{1,0:T(8,128)S(1)} %convolution_add_fusion.24) | copy-start | bytes 393220
  217.9 169.5 %all-reduce.10.cloned.1.call-start = ((), (), s32[]{:S(2)}) async-start(), calls=%async_computation.11 | async-start | bytes 5242880 | tf_op jit(solution)/shard_map/psum | solution.py:91
  388.9 5.6 %copy-start.3 = (f32[256,256]{1,0:T(8,128)}, f32[256,256]{1,0:T(8,128)S(1)}, u32[]{:S(2)}) copy-start(f32[256,256]{1,0:T(8,128)S(1)} %convolution_add_fusion.20) | copy-start | bytes 786436
  (22 other events, 50.7 us)
Sparse Core Ops, SparseCore 0:
  14.5 48.6 all-gather.1
  66.4 49.9 all-reduce.5
  119.4 21.7 reduce-scatter.10
  144.0 19.9 reduce-scatter.8
  166.2 19.8 reduce-scatter.6
  188.3 19.8 reduce-scatter.4
  218.0 105.6 all-reduce.7
  327.1 60.2 all-reduce.9
